TPU v7x, 256 devices: a whole 4x4x8 slice. The times are simulated.
256 devices in a mesh: rep: 2 (over z_hi), dp: 32 (over z_lo, x, core), mp: 4 (over y).
Axes of the slice: x: 4, y: 4, z: 8 (z_hi: 2, z_lo: 4; z = z_hi * 4 + z_lo), core: 2. Of those that a mesh axis runs over, the one named last changes fastest.
Arguments:
- tokens: bfloat16 [24576, 2048], P(('rep', 'dp', 'mp')), may hold values from -6 to 6
- request_ids: int32 [64, 384], P(('rep', 'dp')), may hold values from 0 to 7, never falling along the last dimension, each value on 1 to 192 neighbouring positions
- cache_entries: bfloat16 [32768, 4096], P(('rep', 'dp', 'mp')), may hold values from -250 to 250, as said below
- cached_lengths: int32 [64, 8], replicated, may hold values from 1 to 256, 512 in all within a row
- traded: int32 [32], P('dp'), may hold values from 0 to 1, as said below
- query_weight: bfloat16 [2048, 2048], P(None, 'mp'), may hold values from -0.125 to 0.125
- key_weight: bfloat16 [2048, 2048], P(None, 'mp'), may hold values from -0.125 to 0.125
- value_weight: bfloat16 [2048, 2048], P(None, 'mp'), may hold values from -0.125 to 0.125
- output_weight: bfloat16 [2048, 2048], P('mp'), may hold values from -0.125 to 0.125
- gate_weight: bfloat16 [2048, 8192], P('dp', 'mp'), may hold values from -0.125 to 0.125
- up_weight: bfloat16 [2048, 8192], P('dp', 'mp'), may hold values from -0.125 to 0.125
- down_weight: bfloat16 [2048, 8192], P('dp', 'mp'), may hold values from -0.0625 to 0.0625
Outputs:
- layer_output: bfloat16 [24576, 2048], P(('rep', 'dp', 'mp'))
Inputs may be any that keep to these rules, and one draw needn't show every extreme that they name: `request_ids`: each group's row never falls; every request 0 to 7 has 1 to 192 new tokens in each group, some request exactly 192. `cached_lengths`: each row sums to 512; its largest entry is 256. `traded`: exactly 16 entries are 1. `cache_entries`: keys are stored already rotated to their positions; rows of cache group g are g * 512 to (g + 1) * 512 - 1, the requests' prefixes in request order.
All inputs are finite; a program needn't handle non-finite values.
Results may differ from a plain program's by a relative error of at most 0.013.
The roundings to bfloat16 on the way count: a program that leaves them out, or rounds other values in their place, can miss the bound.
Values may be sent and summed in bfloat16 or wider, within the bound.
A program may use at most 128 MiB of HBM per device.

v0:
```python
import math
import jax
import jax.numpy as jnp
from jax import lax
from jax.sharding import PartitionSpec as P

D = 2048
HEADS = 16
HEAD_DIM = 128
TOK_GROUP = 384
CACHE = 512
EPSILON = 1e-05
ROPE_BASE = 10000.0


def swapped(value, axis, apart):
    mask = 2**apart
    pairs = [(source, source ^ mask) for source in range(lax.axis_size(axis))]
    return lax.ppermute(value, axis, pairs)


def layer_norm(rows):
    center = rows - jnp.mean(rows, axis=-1, keepdims=True)
    spread = jnp.mean(center * center, axis=-1, keepdims=True)
    return center * lax.rsqrt(spread + EPSILON)


def request_layout(request_row, length_row, cache_size):
    number = length_row.shape[0]
    labels = jnp.arange(number, dtype=jnp.int32)
    onehot = (request_row[:, None] == labels[None, :]).astype(jnp.int32)
    counts = jnp.sum(onehot, axis=0)
    starts = jnp.cumsum(counts) - counts
    token_place = jnp.arange(request_row.shape[0], dtype=jnp.int32)
    positions = jnp.sum(onehot * (length_row - starts)[None, :], axis=1) + token_place
    bounds = jnp.cumsum(length_row)
    cache_place = jnp.arange(cache_size, dtype=jnp.int32)
    owner = jnp.sum((cache_place[:, None] >= bounds[None, :]).astype(jnp.int32), axis=1)
    return (positions, owner)


def rotate(vectors, positions):
    half = vectors.shape[-1] // 2
    freq = ROPE_BASE ** (-jnp.arange(half, dtype=jnp.float32) / half)
    angle = positions.astype(jnp.float32)[:, None] * freq[None, :]
    cosine = jnp.cos(angle)[:, None, :]
    sine = jnp.sin(angle)[:, None, :]
    first = vectors[..., :half]
    second = vectors[..., half:]
    return jnp.concatenate(
        [first * cosine - second * sine, second * cosine + first * sine], axis=-1
    )


def attend(query, keys_new, values_new, keys_cache, values_cache, request_row, owner):
    scale = 1.0 / math.sqrt(query.shape[-1])
    keys = jnp.concatenate([keys_cache, keys_new], axis=0)
    values = jnp.concatenate([values_cache, values_new], axis=0)
    scores = jnp.einsum("thd,khd->htk", query, keys, preferred_element_type=jnp.float32) * scale
    count = request_row.shape[0]
    place = jnp.arange(count, dtype=jnp.int32)
    same_cache = owner[None, :] == request_row[:, None]
    same_new = (request_row[None, :] == request_row[:, None]) & (place[None, :] <= place[:, None])
    allowed = jnp.concatenate([same_cache, same_new], axis=1)
    scores = jnp.where(allowed[None], scores, -1e30)
    top = jnp.max(scores, axis=-1, keepdims=True)
    raised = jnp.exp(scores - top)
    total = jnp.sum(raised, axis=-1, keepdims=True)
    weights = (raised / total).astype(jnp.bfloat16)
    mixed = jnp.einsum("htk,khd->thd", weights, values, preferred_element_type=jnp.float32)
    return mixed.astype(jnp.bfloat16)


def local(
    tokens,
    request_ids,
    cache_entries,
    cached_lengths,
    traded,
    query_weight,
    key_weight,
    value_weight,
    output_weight,
    gate_weight,
    up_weight,
    down_weight,
):
    tensor_size = lax.axis_size("mp")
    local_heads = HEADS // tensor_size
    replica = lax.axis_index("rep")
    within = lax.axis_index("dp")
    pairs = lax.axis_size("dp")
    group = replica * pairs + within
    moved_here = traded[0] == 1
    source = jnp.where(moved_here, (1 - replica) * pairs + within, group)
    length_row = lax.dynamic_slice_in_dim(cached_lengths, source, 1, 0)[0]
    request_row = request_ids[0]
    partner = swapped(cache_entries, "rep", 0)
    stored = jnp.where(moved_here, partner, cache_entries)
    by_heads = lax.all_to_all(
        stored.reshape(stored.shape[0], 2, D), "mp", split_axis=2, concat_axis=0, tiled=True
    )
    keys_cache = by_heads[:, 0].reshape(CACHE, local_heads, HEAD_DIM)
    values_cache = by_heads[:, 1].reshape(CACHE, local_heads, HEAD_DIM)
    rows_full = lax.all_gather(tokens, "mp", axis=0, tiled=True)
    positions, owner = request_layout(request_row, length_row, CACHE)
    normed = layer_norm(rows_full.astype(jnp.float32)).astype(jnp.bfloat16)
    query = jnp.dot(normed, query_weight, preferred_element_type=jnp.float32).reshape(
        TOK_GROUP, local_heads, HEAD_DIM
    )
    query = rotate(query, positions).astype(jnp.bfloat16)
    keys_new = jnp.dot(normed, key_weight, preferred_element_type=jnp.float32).reshape(
        TOK_GROUP, local_heads, HEAD_DIM
    )
    keys_new = rotate(keys_new, positions).astype(jnp.bfloat16)
    values_new = (
        jnp.dot(normed, value_weight, preferred_element_type=jnp.float32)
        .astype(jnp.bfloat16)
        .reshape(TOK_GROUP, local_heads, HEAD_DIM)
    )
    mixed = attend(query, keys_new, values_new, keys_cache, values_cache, request_row, owner)
    mixed = mixed.reshape(TOK_GROUP, local_heads * HEAD_DIM)
    own_sum = lax.psum_scatter(
        jnp.dot(mixed, output_weight, preferred_element_type=jnp.float32),
        "mp",
        scatter_dimension=0,
        tiled=True,
    )
    state_own = (tokens.astype(jnp.float32) + own_sum).astype(jnp.bfloat16)
    normed_own = layer_norm(state_own.astype(jnp.float32)).astype(jnp.bfloat16)
    normed_two = lax.all_gather(normed_own, "mp", axis=0, tiled=True)

    def add_rows(piece):
        return jnp.dot(normed_two, piece, preferred_element_type=jnp.float32)

    gate = add_rows(lax.all_gather(gate_weight, "dp", axis=0, tiled=True))
    upward = add_rows(lax.all_gather(up_weight, "dp", axis=0, tiled=True))
    activated = (jax.nn.silu(gate) * upward).astype(jnp.bfloat16)
    terms = lax.dot_general(
        activated,
        lax.all_gather(down_weight, "dp", axis=0, tiled=True),
        (((1,), (1,)), ((), ())),
        preferred_element_type=jnp.float32,
    )
    hidden_own = lax.psum_scatter(terms, "mp", scatter_dimension=0, tiled=True)
    return (state_own.astype(jnp.float32) + hidden_own).astype(jnp.bfloat16)


def solution(mesh):
    in_specs = (
        P(("rep", "dp", "mp"), None),
        P(("rep", "dp"), None),
        P(("rep", "dp", "mp"), None),
        P(),
        P("dp"),
        P(None, "mp"),
        P(None, "mp"),
        P(None, "mp"),
        P("mp", None),
        P("dp", "mp"),
        P("dp", "mp"),
        P("dp", "mp"),
    )
    out_specs = P(("rep", "dp", "mp"), None)
    return jax.shard_map(local, mesh=mesh, in_specs=in_specs, out_specs=out_specs, check_vma=False)
```

profile of v0, /device:TPU:1, one launch (start us, length us, event | category | flops | bytes accessed | tf_op | source)
XLA Modules:
  0.0 476.3 jit_solution(9177185737929228484)
XLA Ops:
  8.3 7.8 %collective-permute-start = (bf16[128,4096]{0,1:T(8,128)(2,1)S(1)}, bf16[128,4096]{0,1:T(8,128)(2,1)}, u32[]{:S(2)}, u32[]{:S(2)}) collective-permute-start(bf16[128,4096]{0,1:T(8,128)(2,1)S(1)} %copy.71), channel_id=1, source_target_pairs={{0,128},{128,0},{1,129},{129,1},{2,130},{130,2},{3,131},{131,3},{4... | collective-permute-start | bytes 3145736 | tf_op jit(solution)/shard_map/ppermute | solution.py:19
  19.2 25.3 %collective-permute-done = bf16[128,4096]{0,1:T(8,128)(2,1)} collective-permute-done((bf16[128,4096]{0,1:T(8,128)(2,1)S(1)}, bf16[128,4096]{0,1:T(8,128)(2,1)}, u32[]{:S(2)}, u32[]{:S(2)}) %collective-permute-start) | collective-permute-done | bytes 1048608 | tf_op jit(solution)/shard_map/ppermute | solution.py:19
  45.9 9.5 %copy.73 = bf16[128,2,2048]{0,1,2:T(2,128)(2,1)} copy(bf16[128,2,2048]{0,2,1:T(8,128)(2,1)S(1)} %bitcast.28) | data formatting | bytes 2097152 | tf_op jit(solution)/shard_map/reshape | solution.py:101
  55.4 4.7 all-to-all-start
  62.5 7.3 %all-to-all-done = bf16[128,2,2048]{0,1,2:T(2,128)(2,1)S(1)} async-done(((bf16[128,2,2048]{0,1,2:T(2,128)(2,1)}), bf16[128,2,2048]{0,1,2:T(2,128)(2,1)S(1)}, u32[]{:S(2)}, u32[]{:S(2)}) %all-to-all-start) | async-done | bytes 1048608 | tf_op jit(solution)/shard_map/all_to_all | solution.py:100
  75.0 2.0 copy.76
  78.9 2.0 fusion.4
  80.8 3.6 fusion.35
  85.8 4.0 fusion.37
  89.8 2.3 reshape.151
  92.1 3.9 convolution_convert_fusion
  95.9 1.9 copy.85
  97.8 2.3 fusion.41
  101.6 2.7 fusion.43
  105.4 2.7 fusion.44
  108.4 61.6 %reduce-scatter.3.cloned.1.call-done = f32[96,2048]{1,0:T(8,128)} async-done(((f32[384,2048]{1,0:T(8,128)}), f32[96,2048]{1,0:T(8,128)}) %reduce-scatter.3.cloned.1.call-update) | async-done | bytes 786448 | tf_op jit(solution)/shard_map/reduce_scatter | solution.py:123
  174.4 27.1 %all-gather.8.cloned.1.call-done = bf16[384,2048]{1,0:T(8,128)(2,1)} async-done(((bf16[96,2048]{1,0:T(8,128)(2,1)}), bf16[384,2048]{1,0:T(8,128)(2,1)}) %all-gather.8.cloned.1.call-update) | async-done | bytes 1572880 | tf_op jit(solution)/shard_map/all_gather | solution.py:131
  201.5 71.4 %all-gather.10.cloned.1.call-done = bf16[2048,2048]{1,0:T(8,128)(2,1)} async-done(((bf16[64,2048]{1,0:T(8,128)(2,1)}), bf16[2048,2048]{1,0:T(8,128)(2,1)}) %all-gather.10.cloned.1.call-update) | async-done | bytes 8388624 | tf_op jit(solution)/shard_map/all_gather | solution.py:136
  272.9 9.0 %fusion.45 = f32[384,2048]{1,0:T(8,128)} fusion(bf16[384,2048]{1,0:T(8,128)(2,1)} %all-gather.8.cloned.1.call-done, bf16[2048,2048]{1,0:T(8,128)(2,1)} %all-gather.10.cloned.1.call-done), kind=kOutput, calls=%fused_computation.76 | convolution fusion | flops 3221225472 | bytes 13107200 | tf_op jit(solution)/shard_map/dot_general | solution.py:134
  281.9 60.6 %all-gather.12.cloned.1.call-done = bf16[2048,2048]{1,0:T(8,128)(2,1)} async-done(((bf16[64,2048]{1,0:T(8,128)(2,1)}), bf16[2048,2048]{1,0:T(8,128)(2,1)}) %all-gather.12.cloned.1.call-update) | async-done | bytes 8388624 | tf_op jit(solution)/shard_map/all_gather | solution.py:137
  342.5 69.7 %all-gather.14.cloned.1.call-done = bf16[2048,2048]{1,0:T(8,128)(2,1)} async-done(((bf16[64,2048]{1,0:T(8,128)(2,1)}), bf16[2048,2048]{1,0:T(8,128)(2,1)}) %all-gather.14.cloned.1.call-update) | async-done | bytes 8388624 | tf_op jit(solution)/shard_map/all_gather | solution.py:141
  412.2 15.9 %fusion.25 = f32[384,2048]{1,0:T(8,128)} fusion(bf16[2048,2048]{1,0:T(8,128)(2,1)} %all-gather.14.cloned.1.call-done, f32[384,2048]{1,0:T(8,128)} %fusion.45, bf16[384,2048]{1,0:T(8,128)(2,1)} %all-gather.8.cloned.1.call-done, bf16[2048,2048]{1,0:T(8,128)(2,1)} %all-gather.12.cloned.1.call-done), kind=kOutput, calls=%fused_computation.42 | convolution fusion | flops 6447169536 | bytes 24641536 | tf_op jit(solution)/shard_map/dot_general | solution.py:139
  428.1 39.4 %reduce-scatter.5.cloned.1.call-done = f32[96,2048]{1,0:T(8,128)} async-done(((f32[384,2048]{1,0:T(8,128)}), f32[96,2048]{1,0:T(8,128)}) %reduce-scatter.5.cloned.1.call-update) | async-done | bytes 786448 | tf_op jit(solution)/shard_map/reduce_scatter | solution.py:145
  467.5 2.0 fusion.24
  (67 shorter events, 23.4 us)
Async XLA Ops:
  6.5 98.8 %copy-start = (bf16[512,2048]{1,0:T(8,128)(2,1)S(1)}, bf16[512,2048]{1,0:T(8,128)(2,1)}, u32[]{:S(2)}) copy-start(bf16[512,2048]{1,0:T(8,128)(2,1)} %param.20) | copy-start | bytes 6291460
  6.5 70.5 %all-gather.6.cloned.1.call-start = ((), (), s32[]{:S(2)}) async-start(), calls=%async_computation.3 | async-start | bytes 1966080 | tf_op jit(solution)/shard_map/all_gather | solution.py:105
  8.3 36.3 %collective-permute-start = (bf16[128,4096]{0,1:T(8,128)(2,1)S(1)}, bf16[128,4096]{0,1:T(8,128)(2,1)}, u32[]{:S(2)}, u32[]{:S(2)}) collective-permute-start(bf16[128,4096]{0,1:T(8,128)(2,1)S(1)} %copy.71), channel_id=1, source_target_pairs={{0,128},{128,0},{1,129},{129,1},{2,130},{130,2},{3,131},{131,3},{4... | collective-permute-start | bytes 3145736 | tf_op jit(solution)/shard_map/ppermute | solution.py:19
  55.4 14.5 %all-to-all-start = ((bf16[128,2,2048]{0,1,2:T(2,128)(2,1)}), bf16[128,2,2048]{0,1,2:T(2,128)(2,1)S(1)}, u32[]{:S(2)}, u32[]{:S(2)}) async-start(bf16[128,2,2048]{0,1,2:T(2,128)(2,1)} %copy.73), calls=%async_computation | async-start | bytes 2097152 | tf_op jit(solution)/shard_map/all_to_all | solution.py:100
  60.1 109.8 %reduce-scatter.3.cloned.1.call-start = ((), (), s32[]{:S(2)}) async-start(), calls=%async_computation.4 | async-start | bytes 3932160 | tf_op jit(solution)/shard_map/reduce_scatter | solution.py:123
  77.0 3.8 copy-start.2
  97.8 2.3 copy-start.4
  97.8 2.3 copy-start.5
  100.6 1.0 copy-start.8
  101.6 2.7 copy-start.6
  101.6 2.7 copy-start.7
  105.4 64.5 %copy-start.3 = (bf16[96,2048]{1,0:T(8,128)(2,1)S(1)}, bf16[96,2048]{1,0:T(8,128)(2,1)}, u32[]{:S(2)}) copy-start(bf16[96,2048]{1,0:T(8,128)(2,1)} %param.12) | copy-start | bytes 1179652
  108.1 93.4 %all-gather.8.cloned.1.call-start = ((), (), s32[]{:S(2)}) async-start(), calls=%async_computation.5 | async-start | bytes 1966080 | tf_op jit(solution)/shard_map/all_gather | solution.py:131
  172.6 100.3 %all-gather.10.cloned.1.call-start = ((), (), s32[]{:S(2)}) async-start(), calls=%async_computation.6 | async-start | bytes 8650752 | tf_op jit(solution)/shard_map/all_gather | solution.py:136
  173.1 169.4 %all-gather.12.cloned.1.call-start = ((), (), s32[]{:S(2)}) async-start(), calls=%async_computation.7 | async-start | bytes 8650752 | tf_op jit(solution)/shard_map/all_gather | solution.py:137
  173.7 238.5 %all-gather.14.cloned.1.call-start = ((), (), s32[]{:S(2)}) async-start(), calls=%async_computation.8 | async-start | bytes 8650752 | tf_op jit(solution)/shard_map/all_gather | solution.py:141
  174.3 293.2 %reduce-scatter.5.cloned.1.call-start = ((), (), s32[]{:S(2)}) async-start(), calls=%async_computation.9 | async-start | bytes 3932160 | tf_op jit(solution)/shard_map/reduce_scatter | solution.py:145
  412.2 57.2 %copy-start.1 = (bf16[512,2048]{1,0:T(8,128)(2,1)S(1)}, bf16[512,2048]{1,0:T(8,128)(2,1)}, u32[]{:S(2)}) copy-start(bf16[512,2048]{1,0:T(8,128)(2,1)} %param.20) | copy-start | bytes 6291460
Sparse Core Ops, SparseCore 0:
  16.3 27.0 all-gather.5
  108.2 61.6 reduce-scatter.2
  172.7 28.7 all-gather.7
  203.2 69.6 all-gather.9
  274.6 67.9 all-gather.11
  344.2 67.9 all-gather.13
  428.2 39.2 reduce-scatter.4
where the time goes:
time: 477 us; the launch traced here: 476 us
  waiting for transfers between devices  364 us (76%)
  matrix products  41 us (9%)
  local copies, waits for them, and re-layouts  27.2 us (6%)
  other arithmetic  16.8 us (4%)
  between operations  14.3 us (3%)
  starting transfers between devices  13 us (3%)
    all_gather x1, waiting for transfers between devices, local(): gate = add_rows(lax.all_gather(gate_weight, 'dp', axis=0, tiled=True))  71.4 us
    all_gather x1, waiting for transfers between devices, local(): lax.all_gather(down_weight, 'dp', axis=0, tiled=True)  69.7 us
    reduce_scatter x1, waiting for transfers between devices, local(): lax.psum_scatter(jnp.dot(mixed, output_weight, preferred_element_type=jnp...  61.6 us
    all_gather x1, waiting for transfers between devices, local(): upward = add_rows(lax.all_gather(up_weight, 'dp', axis=0, tiled=True))  60.6 us
    reduce_scatter x1, waiting for transfers between devices, local(): hidden_own = lax.psum_scatter(terms, 'mp', scatter_dimension=0, tiled=True)  39.4 us
    all_gather x1, waiting for transfers between devices, local(): normed_two = lax.all_gather(normed_own, 'mp', axis=0, tiled=True)  27.1 us
    ppermute x1, waiting for transfers between devices, swapped(): return lax.ppermute(value, axis, pairs)  25.3 us
    dot_general x1, matrix products, local(): lax.dot_general(activated, lax.all_gather(down_weight, 'dp', axis=0, tile...  15.9 us
  transfers between devices with their start and end apart: 9, of which 8 were waited for; matrix products, arithmetic and copies ran while one was open for 7% of the time, Pallas kernels for 0%

commit v1 on v0

--- a/solution.py
+++ b/solution.py
@@ -128,7 +128,21 @@
     )
     state_own = (tokens.astype(jnp.float32) + own_sum).astype(jnp.bfloat16)
     normed_own = layer_norm(state_own.astype(jnp.float32)).astype(jnp.bfloat16)
-    normed_two = lax.all_gather(normed_own, "mp", axis=0, tiled=True)
+    ways, here, lap = (lax.axis_size("mp"), lax.axis_index("mp"), normed_own.shape[0])
+    dims = [n * ways if d == 0 else n for d, n in enumerate(normed_own.shape)]
+    full = lax.dynamic_update_slice_in_dim(
+        jnp.zeros(dims, normed_own.dtype), normed_own, here * lap, axis=0
+    )
+    going_up = going_down = normed_own
+    for far in range(1, ways // 2 + 1):
+        going_up = lax.ppermute(going_up, "mp", [(d, (d + 1) % ways) for d in range(ways)])
+        full = lax.dynamic_update_slice_in_dim(full, going_up, (here - far) % ways * lap, axis=0)
+        if 2 * far < ways:
+            going_down = lax.ppermute(going_down, "mp", [(d, (d - 1) % ways) for d in range(ways)])
+            full = lax.dynamic_update_slice_in_dim(
+                full, going_down, (here + far) % ways * lap, axis=0
+            )
+    normed_two = full
 
     def add_rows(piece):
         return jnp.dot(normed_two, piece, preferred_element_type=jnp.float32)

time: 477 us -> 409 us (0.86)
  waiting for transfers between devices: 364 us -> 293 us
    all_gather x1, waiting for transfers between devices: 71.4 us -> 7.62 us  [local(): gate = add_rows(lax.all_gather(gate_weight, 'dp', axis=0, tiled=True))]
    all_gather x1 -> x0, waiting for transfers between devices: 27.1 us -> none  [local(): normed_two = lax.all_gather(normed_own, 'mp', axis=0, tiled=True)]
    ppermute x0 -> x3, waiting for transfers between devices: none -> 18.8 us  [the longest x2 18.8 us: local(): lax.ppermute(going_up, 'mp', [(d, (d + 1) % ways) for d in range(ways)])]
    all_gather x1, waiting for transfers between devices: 60.6 us -> 70.6 us  [local(): upward = add_rows(lax.all_gather(up_weight, 'dp', axis=0, tiled=True))]
    all_gather x1, waiting for transfers between devices: 69.7 us -> 61.8 us  [local(): lax.all_gather(down_weight, 'dp', axis=0, tiled=True)]
  transfers between devices with their start and end apart: 9 -> 11, of which waited for: 8 -> 9; matrix products, arithmetic and copies ran while one was open for 7% -> 8% of each run, Pallas kernels for 0% -> 0%
where the time goes in v1:
time: 409 us; the launch traced here: 408 us
  waiting for transfers between devices  293 us (72%)
  matrix products  40.6 us (10%)
  local copies, waits for them, and re-layouts  27.5 us (7%)
  other arithmetic  16 us (4%)
  starting transfers between devices  15.7 us (4%)
  between operations  15.7 us (4%)
    all_gather x1, waiting for transfers between devices, local(): upward = add_rows(lax.all_gather(up_weight, 'dp', axis=0, tiled=True))  70.6 us
    all_gather x1, waiting for transfers between devices, local(): lax.all_gather(down_weight, 'dp', axis=0, tiled=True)  61.8 us
    reduce_scatter x1, waiting for transfers between devices, local(): lax.psum_scatter(jnp.dot(mixed, output_weight, preferred_element_type=jnp...  59.8 us
    reduce_scatter x1, waiting for transfers between devices, local(): hidden_own = lax.psum_scatter(terms, 'mp', scatter_dimension=0, tiled=True)  40 us
    ppermute x1, waiting for transfers between devices, swapped(): return lax.ppermute(value, axis, pairs)  25.3 us
    ppermute x2, waiting for transfers between devices, local(): lax.ppermute(going_up, 'mp', [(d, (d + 1) % ways) for d in range(ways)])  18.8 us
    dot_general x1, matrix products, local(): lax.dot_general(activated, lax.all_gather(down_weight, 'dp', axis=0, tile...  15.9 us
    reshape x1, local copies, waits for them, and re-layouts, local(): stored.reshape(stored.shape[0], 2, D)  9.46 us
  transfers between devices with their start and end apart: 11, of which 9 were waited for; matrix products, arithmetic and copies ran while one was open for 8% of the time, Pallas kernels for 0%

profile of v1, /device:TPU:1, one launch (start us, length us, event | category | flops | bytes accessed | tf_op | source)
XLA Modules:
  0.0 408.4 jit_solution(12269917901234225970)
XLA Ops:
  9.1 7.8 %collective-permute-start = (bf16[128,4096]{0,1:T(8,128)(2,1)S(1)}, bf16[128,4096]{0,1:T(8,128)(2,1)}, u32[]{:S(2)}, u32[]{:S(2)}) collective-permute-start(bf16[128,4096]{0,1:T(8,128)(2,1)S(1)} %copy.71), channel_id=1, source_target_pairs={{0,128},{128,0},{1,129},{129,1},{2,130},{130,2},{3,131},{131,3},{4... | collective-permute-start | bytes 3145736 | tf_op jit(solution)/shard_map/ppermute | solution.py:19
  20.1 25.3 %collective-permute-done = bf16[128,4096]{0,1:T(8,128)(2,1)} collective-permute-done((bf16[128,4096]{0,1:T(8,128)(2,1)S(1)}, bf16[128,4096]{0,1:T(8,128)(2,1)}, u32[]{:S(2)}, u32[]{:S(2)}) %collective-permute-start) | collective-permute-done | bytes 1048608 | tf_op jit(solution)/shard_map/ppermute | solution.py:19
  46.7 9.5 %copy.73 = bf16[128,2,2048]{0,1,2:T(2,128)(2,1)} copy(bf16[128,2,2048]{0,2,1:T(8,128)(2,1)S(1)} %bitcast.28) | data formatting | bytes 2097152 | tf_op jit(solution)/shard_map/reshape | solution.py:101
  56.2 4.7 %all-to-all-start = ((bf16[128,2,2048]{0,1,2:T(2,128)(2,1)}), bf16[128,2,2048]{0,1,2:T(2,128)(2,1)S(1)}, u32[]{:S(2)}, u32[]{:S(2)}) async-start(bf16[128,2,2048]{0,1,2:T(2,128)(2,1)} %copy.73), calls=%async_computation | async-start | bytes 2097152 | tf_op jit(solution)/shard_map/all_to_all | solution.py:100
  63.3 7.3 %all-to-all-done = bf16[128,2,2048]{0,1,2:T(2,128)(2,1)S(1)} async-done(((bf16[128,2,2048]{0,1,2:T(2,128)(2,1)}), bf16[128,2,2048]{0,1,2:T(2,128)(2,1)S(1)}, u32[]{:S(2)}, u32[]{:S(2)}) %all-to-all-start) | async-done | bytes 1048608 | tf_op jit(solution)/shard_map/all_to_all | solution.py:100
  75.8 2.0 copy.76
  81.7 3.5 fusion.38
  86.6 4.0 fusion.36
  90.6 2.3 reshape.153
  92.9 3.9 convolution_convert_fusion
  98.7 2.3 fusion.43
  102.4 2.7 fusion.45
  106.2 2.8 fusion.48
  111.0 59.8 %reduce-scatter.3.cloned.1.call-done = f32[96,2048]{1,0:T(8,128)} async-done(((f32[384,2048]{1,0:T(8,128)}), f32[96,2048]{1,0:T(8,128)}) %reduce-scatter.3.cloned.1.call-update) | async-done | bytes 786448 | tf_op jit(solution)/shard_map/reduce_scatter | solution.py:123
  173.0 2.7 collective-permute-start.2
  175.6 8.6 %collective-permute-done.1 = bf16[96,2048]{1,0:T(8,128)(2,1)S(1)} collective-permute-done((bf16[96,2048]{1,0:T(8,128)(2,1)S(1)}, bf16[96,2048]{1,0:T(8,128)(2,1)S(1)}, u32[]{:S(2)}, u32[]{:S(2)}) %collective-permute-start.1) | collective-permute-done | bytes 393248 | tf_op jit(solution)/shard_map/ppermute | solution.py:138
  184.3 10.2 %collective-permute-done.3 = bf16[96,2048]{1,0:T(8,128)(2,1)S(1)} collective-permute-done((bf16[96,2048]{1,0:T(8,128)(2,1)S(1)}, bf16[96,2048]{1,0:T(8,128)(2,1)S(1)}, u32[]{:S(2)}, u32[]{:S(2)}) %collective-permute-start.3) | collective-permute-done | bytes 393248 | tf_op jit(solution)/shard_map/ppermute | solution.py:138
  194.6 7.6 %all-gather.7.cloned.1.call-done = bf16[2048,2048]{1,0:T(8,128)(2,1)} async-done(((bf16[64,2048]{1,0:T(8,128)(2,1)}), bf16[2048,2048]{1,0:T(8,128)(2,1)}) %all-gather.7.cloned.1.call-update) | async-done | bytes 8388624 | tf_op jit(solution)/shard_map/all_gather | solution.py:150
  202.2 8.5 %fusion.49 = f32[384,2048]{1,0:T(8,128)} fusion(bf16[384,2048]{1,0:T(8,128)(2,1)S(1)} %constant_dynamic-update-slice_fusion, bf16[2048,2048]{1,0:T(8,128)(2,1)} %all-gather.7.cloned.1.call-done), kind=kOutput, calls=%fused_computation.82 | convolution fusion | flops 3221225472 | bytes 13107200 | tf_op jit(solution)/shard_map/dot_general | solution.py:148
  210.7 61.8 %all-gather.11.cloned.1.call-done = bf16[2048,2048]{1,0:T(8,128)(2,1)} async-done(((bf16[64,2048]{1,0:T(8,128)(2,1)}), bf16[2048,2048]{1,0:T(8,128)(2,1)}) %all-gather.11.cloned.1.call-update) | async-done | bytes 8388624 | tf_op jit(solution)/shard_map/all_gather | solution.py:155
  272.6 70.6 %all-gather.9.cloned.1.call-done = bf16[2048,2048]{1,0:T(8,128)(2,1)} async-done(((bf16[64,2048]{1,0:T(8,128)(2,1)}), bf16[2048,2048]{1,0:T(8,128)(2,1)}) %all-gather.9.cloned.1.call-update) | async-done | bytes 8388624 | tf_op jit(solution)/shard_map/all_gather | solution.py:151
  343.2 15.9 %fusion.10 = f32[384,2048]{1,0:T(8,128)} fusion(bf16[2048,2048]{1,0:T(8,128)(2,1)} %all-gather.11.cloned.1.call-done, f32[384,2048]{1,0:T(8,128)} %fusion.49, bf16[384,2048]{1,0:T(8,128)(2,1)} %copy-done.3, bf16[2048,2048]{1,0:T(8,128)(2,1)} %all-gather.9.cloned.1.call-done), kind=kOutput, calls=%fused_computation.16 | convolution fusion | flops 6447169536 | bytes 24641536 | tf_op jit(solution)/shard_map/dot_general | solution.py:153
  359.1 40.0 %reduce-scatter.5.cloned.1.call-done = f32[96,2048]{1,0:T(8,128)} async-done(((f32[384,2048]{1,0:T(8,128)}), f32[96,2048]{1,0:T(8,128)}) %reduce-scatter.5.cloned.1.call-update) | async-done | bytes 786448 | tf_op jit(solution)/shard_map/reduce_scatter | solution.py:159
  399.1 2.0 fusion.26
  (76 shorter events, 26.8 us)
Async XLA Ops:
  7.4 98.9 %copy-start = (bf16[512,2048]{1,0:T(8,128)(2,1)S(1)}, bf16[512,2048]{1,0:T(8,128)(2,1)}, u32[]{:S(2)}) copy-start(bf16[512,2048]{1,0:T(8,128)(2,1)} %param.20) | copy-start | bytes 6291460
  7.4 70.5 %all-gather.5.cloned.1.call-start = ((), (), s32[]{:S(2)}) async-start(), calls=%async_computation.3 | async-start | bytes 1966080 | tf_op jit(solution)/shard_map/all_gather | solution.py:105
  9.1 36.3 %collective-permute-start = (bf16[128,4096]{0,1:T(8,128)(2,1)S(1)}, bf16[128,4096]{0,1:T(8,128)(2,1)}, u32[]{:S(2)}, u32[]{:S(2)}) collective-permute-start(bf16[128,4096]{0,1:T(8,128)(2,1)S(1)} %copy.71), channel_id=1, source_target_pairs={{0,128},{128,0},{1,129},{129,1},{2,130},{130,2},{3,131},{131,3},{4... | collective-permute-start | bytes 3145736 | tf_op jit(solution)/shard_map/ppermute | solution.py:19
  56.2 14.5 %all-to-all-start = ((bf16[128,2,2048]{0,1,2:T(2,128)(2,1)}), bf16[128,2,2048]{0,1,2:T(2,128)(2,1)S(1)}, u32[]{:S(2)}, u32[]{:S(2)}) async-start(bf16[128,2,2048]{0,1,2:T(2,128)(2,1)} %copy.73), calls=%async_computation | async-start | bytes 2097152 | tf_op jit(solution)/shard_map/all_to_all | solution.py:100
  60.9 109.9 %reduce-scatter.3.cloned.1.call-start = ((), (), s32[]{:S(2)}) async-start(), calls=%async_computation.4 | async-start | bytes 3932160 | tf_op jit(solution)/shard_map/reduce_scatter | solution.py:123
  77.9 3.8 copy-start.2
  98.7 2.3 copy-start.5
  98.7 2.3 copy-start.6
  101.4 1.0 copy-start.9
  102.4 2.7 copy-start.7
  102.4 2.7 copy-start.8
  109.0 61.8 %copy-start.4 = (bf16[96,2048]{1,0:T(8,128)(2,1)S(1)}, bf16[96,2048]{1,0:T(8,128)(2,1)}, u32[]{:S(2)}) copy-start(bf16[96,2048]{1,0:T(8,128)(2,1)} %param.12) | copy-start | bytes 1179652
  109.0 93.2 %all-gather.7.cloned.1.call-start = ((), (), s32[]{:S(2)}) async-start(), calls=%async_computation.5 | async-start | bytes 8650752 | tf_op jit(solution)/shard_map/all_gather | solution.py:150
  109.6 163.0 %all-gather.11.cloned.1.call-start = ((), (), s32[]{:S(2)}) async-start(), calls=%async_computation.7 | async-start | bytes 8650752 | tf_op jit(solution)/shard_map/all_gather | solution.py:155
  110.2 233.0 %all-gather.9.cloned.1.call-start = ((), (), s32[]{:S(2)}) async-start(), calls=%async_computation.6 | async-start | bytes 8650752 | tf_op jit(solution)/shard_map/all_gather | solution.py:151
  110.8 288.3 %reduce-scatter.5.cloned.1.call-start = ((), (), s32[]{:S(2)}) async-start(), calls=%async_computation.8 | async-start | bytes 3932160 | tf_op jit(solution)/shard_map/reduce_scatter | solution.py:159
  172.9 11.3 %collective-permute-start.1 = (bf16[96,2048]{1,0:T(8,128)(2,1)S(1)}, bf16[96,2048]{1,0:T(8,128)(2,1)S(1)}, u32[]{:S(2)}, u32[]{:S(2)}) collective-permute-start(bf16[96,2048]{1,0:T(8,128)(2,1)S(1)} %get-tuple-element.6), channel_id=1, source_target_pairs={{0,1},{1,2},{2,3},{3,0},{4,5},{5,6},{6,7},{7,4},{8,9},{9,10},{10,1... | collective-permute-start | bytes 1179656 | tf_op jit(solution)/shard_map/ppermute | solution.py:138
  173.0 11.3 %collective-permute-start.2 = (bf16[96,2048]{1,0:T(8,128)(2,1)S(1)}, bf16[96,2048]{1,0:T(8,128)(2,1)S(1)}, u32[]{:S(2)}, u32[]{:S(2)}) collective-permute-start(bf16[96,2048]{1,0:T(8,128)(2,1)S(1)} %get-tuple-element.6), channel_id=1, source_target_pairs={{0,3},{1,0},{2,1},{3,2},{4,7},{5,4},{6,5},{7,6},{8,11},{9,8},{10,9... | collective-permute-start | bytes 1179656 | tf_op jit(solution)/shard_map/ppermute | solution.py:141
  184.2 10.3 %collective-permute-start.3 = (bf16[96,2048]{1,0:T(8,128)(2,1)S(1)}, bf16[96,2048]{1,0:T(8,128)(2,1)S(1)}, u32[]{:S(2)}, u32[]{:S(2)}) collective-permute-start(bf16[96,2048]{1,0:T(8,128)(2,1)S(1)} %collective-permute-done.1), channel_id=1, source_target_pairs={{0,1},{1,2},{2,3},{3,0},{4,5},{5,6},{6,7},{7,4},{8,9},{9,10},{10,1... | collective-permute-start | bytes 1179656 | tf_op jit(solution)/shard_map/ppermute | solution.py:138
  194.6 16.2 %copy-start.3 = (bf16[384,2048]{1,0:T(8,128)(2,1)}, bf16[384,2048]{1,0:T(8,128)(2,1)S(1)}, u32[]{:S(2)}) copy-start(bf16[384,2048]{1,0:T(8,128)(2,1)S(1)} %constant_dynamic-update-slice_fusion) | copy-start | bytes 4718596
  343.2 57.8 %copy-start.1 = (bf16[512,2048]{1,0:T(8,128)(2,1)S(1)}, bf16[512,2048]{1,0:T(8,128)(2,1)}, u32[]{:S(2)}) copy-start(bf16[512,2048]{1,0:T(8,128)(2,1)} %param.20) | copy-start | bytes 6291460
Sparse Core Ops, SparseCore 0:
  17.1 27.0 all-gather.4
  109.1 61.6 reduce-scatter.2
  359.2 39.8 reduce-scatter.4
Sparse Core Ops, SparseCore 1:
  111.4 90.8 all-gather.6
  203.9 68.6 all-gather.10
  274.3 68.9 all-gather.8
